TPU v7x, 32 devices: a whole 2x2x4 slice. The times are simulated.
32 devices in a mesh: dp: 8 (over z, x), mp: 4 (over y, core).
Axes of the slice: x: 2, y: 2, z: 4, core: 2. Of those that a mesh axis runs over, the one named last changes fastest.
Arguments:
- hidden_in: bfloat16 [16384, 768], P(('dp', 'mp')), may hold values from -6 to 6
- box_coords: int32 [16384, 4], P(('dp', 'mp')), may hold values from 0 to 999
- page_lengths: int32 [32, 6], P('dp'), may hold values from 1 to 400, 480 in all within a row
- qkv_weight: bfloat16 [768, 3, 768], P(None, None, 'mp'), may hold values from -0.21875 to 0.21875
- box_weight: bfloat16 [128, 768], P(None, 'mp'), may hold values from -0.75 to 0.75
- out_weight: bfloat16 [768, 768], P('mp'), may hold values from -0.875 to 0.875
- norm1_gain: float32 [768], replicated, may hold values from 0.5 to 1.5
- norm1_bias: float32 [768], replicated, may hold values from -1 to 1
- up_weight: bfloat16 [768, 3072], P(None, 'mp'), may hold values from -0.21875 to 0.21875
- up_bias: bfloat16 [3072], P('mp'), may hold values from -1.5 to 1.5
- down_weight: bfloat16 [3072, 768], P('mp'), may hold values from -0.15625 to 0.15625
- norm2_gain: float32 [768], replicated, may hold values from 0.5 to 1.5
- norm2_bias: float32 [768], replicated, may hold values from -1 to 1
- out_grad: bfloat16 [16384, 768], P(('dp', 'mp')), may hold values from -6 to 6
Outputs:
- layer_out: bfloat16 [16384, 768], P(('dp', 'mp'))
- input_grad: float32 [16384, 768], P(('dp', 'mp'))
- qkv_weight_grad: float32 [768, 3, 768], P(None, None, 'mp')
- box_weight_grad: float32 [128, 768], P(None, 'mp')
- out_weight_grad: float32 [768, 768], P('mp')
- norm1_gain_grad: float32 [768], replicated
- norm1_bias_grad: float32 [768], replicated
- up_weight_grad: float32 [768, 3072], P(None, 'mp')
- up_bias_grad: float32 [3072], P('mp')
- down_weight_grad: float32 [3072, 768], P('mp')
- norm2_gain_grad: float32 [768], replicated
- norm2_bias_grad: float32 [768], replicated
Inputs may be any that keep to these rules, and one draw needn't show every extreme that they name: `page_lengths`: each slot's 6 lengths sum to 480; the slot's remaining positions are padding.
All inputs are finite; a program needn't handle non-finite values.
Results may differ from a plain program's by a relative error of at most 0.015.
The roundings to bfloat16 on the way count: a program that leaves them out, or rounds other values in their place, can miss the bound.
Values may be sent and summed in bfloat16 or wider, within the bound.
A program may use at most 128 MiB of HBM per device.

v0:
```python
import jax
import jax.numpy as jnp
from jax import lax
from jax.sharding import PartitionSpec as P

HEAD_DIM = 64
SLOT_LEN = 512


EPSILON = 1e-05
MASKED = -1000000000.0
ROOT_HALF = 0.7071067811865476
INV_ROOT_TAU = 0.3989422804014327


def box_features(box_coords, feat_width):
    freq_count = feat_width // 8
    frequency = jnp.exp(-jnp.log(10000.0) * jnp.arange(freq_count, dtype=jnp.float32) / freq_count)
    angles = box_coords.astype(jnp.float32)[:, :, None] * frequency[None, None, :]
    angles = angles.reshape(box_coords.shape[0], 4 * freq_count)
    return jnp.concatenate([jnp.cos(angles), jnp.sin(angles)], axis=1)


def segments(lengths):
    page_ends = jnp.cumsum(lengths)
    position = jnp.arange(SLOT_LEN, dtype=jnp.int32)
    return jnp.sum((position[:, None] >= page_ends[None, :]).astype(jnp.int32), axis=1)


def norm_forward(values, norm_gain, norm_bias):
    row_mean = jnp.mean(values, axis=-1, keepdims=True)
    centred = values - row_mean
    inv_dev = lax.rsqrt(jnp.mean(centred * centred, axis=-1, keepdims=True) + EPSILON)
    scaled = centred * inv_dev
    return (scaled * norm_gain + norm_bias, scaled, inv_dev)


def norm_backward(upstream, scaled, inv_dev, norm_gain):
    weighted = upstream * norm_gain
    back = inv_dev * (
        weighted
        - jnp.mean(weighted, axis=-1, keepdims=True)
        - scaled * jnp.mean(weighted * scaled, axis=-1, keepdims=True)
    )
    return (back, jnp.sum(upstream * scaled, axis=0), jnp.sum(upstream, axis=0))


def gelu_exact(values):
    return 0.5 * values * (1.0 + lax.erf(values * ROOT_HALF))


def gelu_slope(values):
    return (
        0.5 * (1.0 + lax.erf(values * ROOT_HALF))
        + values * jnp.exp(-0.5 * values * values) * INV_ROOT_TAU
    )


def slot_scores(query_block, key_block, id_block, score_scale):
    raw_scores = (
        jnp.einsum("ihe,jhe->hij", query_block, key_block, preferred_element_type=jnp.float32)
        * score_scale
    )
    same_page = id_block[:, None] == id_block[None, :]
    return jnp.where(same_page[None], raw_scores, MASKED)


def on_device(
    hidden_in,
    box_coords,
    page_lengths,
    qkv_weight,
    box_weight,
    out_weight,
    norm1_gain,
    norm1_bias,
    up_weight,
    up_bias,
    down_weight,
    norm2_gain,
    norm2_bias,
    out_grad,
):
    local_width = qkv_weight.shape[2]
    feat_width = box_weight.shape[0]
    half_width = feat_width // 2
    head_count = local_width // HEAD_DIM
    slot_count = page_lengths.shape[0]
    aug_width = HEAD_DIM + feat_width
    score_scale = HEAD_DIM ** (-0.5)
    features = box_features(box_coords, feat_width).astype(jnp.bfloat16)
    whole_x, whole_feats = (
        lax.all_gather(hidden_in, "mp", axis=0, tiled=True),
        lax.all_gather(features, "mp", axis=0, tiled=True),
    )
    group_rows = whole_x.shape[0]
    projected = jnp.einsum("nd,dce->nce", whole_x, qkv_weight, preferred_element_type=jnp.float32)
    queries = projected[:, 0].astype(jnp.bfloat16).reshape(group_rows, head_count, HEAD_DIM)
    key_rows = projected[:, 1].astype(jnp.bfloat16).reshape(group_rows, head_count, HEAD_DIM)
    value_rows = projected[:, 2].astype(jnp.bfloat16).reshape(group_rows, head_count, HEAD_DIM)
    box_heads = box_weight.reshape(feat_width, head_count, HEAD_DIM)
    box_turn = jnp.einsum("nhe,phe->nhp", queries, box_heads, preferred_element_type=jnp.float32)
    cosine = whole_feats[:, None, :half_width].astype(jnp.float32)
    sine_part = whole_feats[:, None, half_width:].astype(jnp.float32)
    sin_coef = box_turn[..., :half_width]
    cos_coef = box_turn[..., half_width:]
    rotated = jnp.concatenate(
        [sin_coef * sine_part + cos_coef * cosine, cos_coef * sine_part - sin_coef * cosine],
        axis=-1,
    ).astype(jnp.bfloat16)
    page_ids = jax.vmap(segments)(page_lengths)
    query_aug = jnp.concatenate([queries, rotated], axis=-1).reshape(
        slot_count, SLOT_LEN, head_count, aug_width
    )
    key_aug = jnp.concatenate(
        [key_rows, jnp.broadcast_to(whole_feats[:, None, :], (group_rows, head_count, feat_width))],
        axis=-1,
    ).reshape(slot_count, SLOT_LEN, head_count, aug_width)
    value_slots = value_rows.reshape(slot_count, SLOT_LEN, head_count, HEAD_DIM)

    def attend(inputs):
        query_block, key_block, value_block, id_block = inputs
        scores = slot_scores(query_block, key_block, id_block, score_scale)
        row_max = jnp.max(scores, axis=-1, keepdims=True)
        exp_terms = jnp.exp(scores - row_max)
        row_total = jnp.sum(exp_terms, axis=-1, keepdims=True)
        probability = (exp_terms / row_total).astype(jnp.bfloat16)
        context_block = jnp.einsum(
            "hij,jhe->ihe", probability, value_block, preferred_element_type=jnp.float32
        )
        return (context_block.astype(jnp.bfloat16), row_max[..., 0] + jnp.log(row_total[..., 0]))

    context, log_total = lax.map(attend, (query_aug, key_aug, value_slots, page_ids))
    context = context.reshape(group_rows, local_width)
    row_part = context
    attended = lax.psum_scatter(
        jnp.dot(row_part, out_weight, preferred_element_type=jnp.float32),
        "mp",
        scatter_dimension=0,
        tiled=True,
    )
    normed, scaled_one, inv_one = norm_forward(
        hidden_in.astype(jnp.float32) + attended, norm1_gain, norm1_bias
    )
    normed_low = normed.astype(jnp.bfloat16)
    full_up, full_bias, full_down = (
        lax.all_gather(up_weight, "mp", axis=1, tiled=True),
        lax.all_gather(up_bias, "mp", axis=0, tiled=True),
        lax.all_gather(down_weight, "mp", axis=0, tiled=True),
    )
    ffn_pre = jnp.dot(normed_low, full_up, preferred_element_type=jnp.float32) + full_bias.astype(
        jnp.float32
    )
    active = gelu_exact(ffn_pre).astype(jnp.bfloat16)
    branch = jnp.dot(active, full_down, preferred_element_type=jnp.float32)
    layer_pre, scaled_two, inv_two = norm_forward(normed + branch, norm2_gain, norm2_bias)
    layer_out = layer_pre.astype(jnp.bfloat16)
    pre2_grad, gain2_part, bias2_part = norm_backward(
        out_grad.astype(jnp.float32), scaled_two, inv_two, norm2_gain
    )
    branch_grad = pre2_grad.astype(jnp.bfloat16)
    active_grad = jnp.einsum(
        "nd,fd->nf", branch_grad, full_down, preferred_element_type=jnp.float32
    )
    ffn_grad = (active_grad * gelu_slope(ffn_pre)).astype(jnp.bfloat16)
    up_part = jnp.einsum("nd,nf->df", normed_low, ffn_grad, preferred_element_type=jnp.float32)
    bias_part = jnp.sum(ffn_grad.astype(jnp.float32), axis=0)
    down_part = jnp.einsum("nf,nd->fd", active, branch_grad, preferred_element_type=jnp.float32)
    up_grad, up_bias_grad, down_grad = (
        lax.psum_scatter(up_part, "mp", scatter_dimension=1, tiled=True),
        lax.psum_scatter(bias_part, "mp", scatter_dimension=0, tiled=True),
        lax.psum_scatter(down_part, "mp", scatter_dimension=0, tiled=True),
    )
    normed_back = jnp.einsum("nf,df->nd", ffn_grad, full_up, preferred_element_type=jnp.float32)
    pre1_grad, gain1_part, bias1_part = norm_backward(
        pre2_grad + normed_back, scaled_one, inv_one, norm1_gain
    )
    whole_attn_grad = lax.all_gather(pre1_grad.astype(jnp.bfloat16), "mp", axis=0, tiled=True)
    out_grad_weight = jnp.einsum(
        "nc,nd->cd", context, whole_attn_grad, preferred_element_type=jnp.float32
    )
    context_grad = jnp.einsum(
        "nd,cd->nc", whole_attn_grad, out_weight, preferred_element_type=jnp.float32
    ).astype(jnp.bfloat16)
    context_grad = context_grad.reshape(slot_count, SLOT_LEN, head_count, HEAD_DIM)

    def attend_back(inputs):
        query_block, key_block, value_block, id_block, log_block, upstream = inputs
        scores = slot_scores(query_block, key_block, id_block, score_scale)
        probability = jnp.exp(scores - log_block[..., None])
        prob_low = probability.astype(jnp.bfloat16)
        value_grad = jnp.einsum(
            "hij,ihe->jhe", prob_low, upstream, preferred_element_type=jnp.float32
        )
        prob_grad = jnp.einsum(
            "ihe,jhe->hij", upstream, value_block, preferred_element_type=jnp.float32
        )
        row_dot = jnp.sum(prob_grad * probability, axis=-1, keepdims=True)
        score_grad = (probability * (prob_grad - row_dot)).astype(jnp.bfloat16)
        aug_grad = (
            jnp.einsum("hij,jhe->ihe", score_grad, key_block, preferred_element_type=jnp.float32)
            * score_scale
        )
        key_grad = (
            jnp.einsum(
                "hij,ihe->jhe",
                score_grad,
                query_block[..., :HEAD_DIM],
                preferred_element_type=jnp.float32,
            )
            * score_scale
        )
        return (aug_grad, key_grad.astype(jnp.bfloat16), value_grad.astype(jnp.bfloat16))

    aug_grad, key_grad, value_grad = lax.map(
        attend_back, (query_aug, key_aug, value_slots, page_ids, log_total, context_grad)
    )
    aug_grad = aug_grad.reshape(group_rows, head_count, aug_width)
    query_part = aug_grad[..., :HEAD_DIM]
    rot_cos = aug_grad[..., HEAD_DIM : HEAD_DIM + half_width]
    rot_sin = aug_grad[..., HEAD_DIM + half_width :]
    turn_grad = jnp.concatenate(
        [rot_cos * sine_part - rot_sin * cosine, rot_cos * cosine + rot_sin * sine_part], axis=-1
    ).astype(jnp.bfloat16)
    box_grad = jnp.einsum(
        "nhp,nhe->phe", turn_grad, queries, preferred_element_type=jnp.float32
    ).reshape(feat_width, local_width)
    query_grad = (
        query_part
        + jnp.einsum("nhp,phe->nhe", turn_grad, box_heads, preferred_element_type=jnp.float32)
    ).astype(jnp.bfloat16)
    stacked_grad = jnp.stack(
        [
            query_grad.reshape(group_rows, local_width),
            key_grad.reshape(group_rows, local_width),
            value_grad.reshape(group_rows, local_width),
        ],
        axis=1,
    )
    qkv_grad = jnp.einsum("nd,nce->dce", whole_x, stacked_grad, preferred_element_type=jnp.float32)
    row_part = stacked_grad
    input_grad = pre1_grad + lax.psum_scatter(
        jnp.einsum("nce,dce->nd", row_part, qkv_weight, preferred_element_type=jnp.float32),
        "mp",
        scatter_dimension=0,
        tiled=True,
    )
    gain1_grad, bias1_grad, gain2_grad, bias2_grad = lax.psum(
        (gain1_part, bias1_part, gain2_part, bias2_part), ("dp", "mp")
    )
    qkv_grad, box_grad, out_grad_weight, up_grad, up_bias_grad, down_grad = lax.psum(
        (qkv_grad, box_grad, out_grad_weight, up_grad, up_bias_grad, down_grad), "dp"
    )
    return (
        layer_out,
        input_grad,
        qkv_grad,
        box_grad,
        out_grad_weight,
        gain1_grad,
        bias1_grad,
        up_grad,
        up_bias_grad,
        down_grad,
        gain2_grad,
        bias2_grad,
    )


def solution(mesh):
    in_specs = (
        P(("dp", "mp"), None),
        P(("dp", "mp"), None),
        P("dp", None),
        P(None, None, "mp"),
        P(None, "mp"),
        P("mp", None),
        P(),
        P(),
        P(None, "mp"),
        P("mp"),
        P("mp", None),
        P(),
        P(),
        P(("dp", "mp"), None),
    )
    out_specs = (
        P(("dp", "mp"), None),
        P(("dp", "mp"), None),
        P(None, None, "mp"),
        P(None, "mp"),
        P("mp", None),
        P(),
        P(),
        P(None, "mp"),
        P("mp"),
        P("mp", None),
        P(),
        P(),
    )
    return jax.shard_map(
        on_device, mesh=mesh, in_specs=in_specs, out_specs=out_specs, check_vma=False
    )
```

profile of v0, /device:TPU:0, one launch (start us, length us, event | category | flops | bytes accessed | tf_op | source)
XLA Modules:
  0.0 779.7 jit_solution(6978596298470826969)
XLA Ops:
  9.4 8.6 %all_gather.19 = bf16[2048,128]{0,1:T(8,128)(2,1)S(1)} all-gather(bf16[512,128]{0,1:T(8,128)(2,1)S(1)} %pad_maximum_fusion.7), channel_id=1, replica_groups=mesh['dp'=8,'mp'=4] {'mp'}, dimensions={0}, use_global_device_ids=true | all-gather | bytes 655360 | tf_op jit(solution)/shard_map/all_gather | solution.py:94
  19.9 20.9 %all-gather.6.cloned.1.call-done = bf16[2048,768]{1,0:T(8,128)(2,1)} async-done(((bf16[512,768]{1,0:T(8,128)(2,1)}), bf16[2048,768]{1,0:T(8,128)(2,1)}) %all-gather.6.cloned.1.call-update) | async-done | bytes 3145744 | tf_op jit(solution)/shard_map/all_gather | solution.py:93
  40.9 3.9 fusion.91
  48.3 2.7 fusion.89
  51.0 2.3 convert_element_type.112
  54.3 2.3 convert_element_type.104
  62.8 24.4 %while.26 = (s32[]{:T(128)}, bf16[4,512,3,64]{1,3,2,0:T(8,128)(2,1)}, f32[4,3,512]{2,1,0:T(4,128)}, bf16[4,512,3,64]{1,3,2,0:T(8,128)(2,1)}, s32[4,512]{1,0:T(4,...) while((s32[]{:T(128)}, ...), condition=%wide.region_5.6_spmd, body=%wide.region_2.5_spmd.sunk | while | flops 412449280 | bytes 12118617 | solution.py:133
  66.2 2.7 fusion.134
  72.3 2.7 fusion.134
  78.4 2.7 fusion.134
  84.5 2.7 fusion.134
  87.2 2.4 copy.90
  90.6 3.7 fusion.92
  95.7 5.2 all-gather
  101.5 51.3 %reduce-scatter.5.cloned.1.call-done = f32[512,768]{1,0:T(8,128)} async-done(((f32[2048,768]{1,0:T(8,128)}), f32[512,768]{1,0:T(8,128)}) %reduce-scatter.5.cloned.1.call-update) | async-done | bytes 1572880 | tf_op jit(solution)/shard_map/reduce_scatter | solution.py:136
  154.8 37.2 %all-gather.8.cloned.1.call-done = bf16[768,3072]{1,0:T(8,128)(2,1)} async-done(((bf16[768,768]{1,0:T(8,128)(2,1)}), bf16[768,3072]{1,0:T(8,128)(2,1)}) %all-gather.8.cloned.1.call-update) | async-done | bytes 4718608 | tf_op jit(solution)/shard_map/all_gather | solution.py:147
  192.0 8.2 %multiply_convert_fusion.1 = (bf16[512,3072]{1,0:T(8,128)(2,1)}, f32[512,3072]{1,0:T(8,128)}) fusion(f32[3072]{0:T(1024)} %bitcast.209, bf16[768,3072]{1,0:T(8,128)(2,1)} %all-gather.8.cloned.1.call-done, f32[512,768]{1,0:T(8,128)S(1)} %get-tuple-element.231, f32[768]{0:T(1024)} %param.25, f32[768]{0:T(1024)} %param.24, f32[512]{0:T(512)S(1)} %add_rsqrt_fusion.1, ...), kind=kOutput, calls=%fused_computation.65 | convolution fusion | flops 2427322368 | bytes 15751168 | tf_op jit(solution)/shard_map/dot_general | solution.py:151
  200.1 30.8 %all-gather.10.cloned.1.call-done = bf16[3072,768]{1,0:T(8,128)(2,1)} async-done(((bf16[768,768]{1,0:T(8,128)(2,1)}), bf16[3072,768]{1,0:T(8,128)(2,1)}) %all-gather.10.cloned.1.call-update) | async-done | bytes 4718608 | tf_op jit(solution)/shard_map/all_gather | solution.py:149
  231.0 6.2 fusion.90
  237.6 2.2 fusion.64
  240.4 7.9 %convert_reduce_fusion = (f32[3072]{0:T(1024)}, bf16[512,3072]{1,0:T(8,128)(2,1)S(1)}) fusion(f32[512,3072]{1,0:T(8,128)S(1)} %copy-done.60, f32[3072]{0:T(1024)S(1)} %bitcast.210, bf16[3072,768]{1,0:T(8,128)(2,1)S(1)} %copy-done.55, f32[512]{0:T(512)S(1)} %get-tuple-element.254, f32[512,768]{1,0:T(8,128)S(1)} %get-tuple-element.250, ...), kind=kOutput, calls=%fused_computation.64 | convolution fusion | flops 2439902208 | bytes 16550912 | tf_op jit(solution)/shard_map/nd,fd->nf/dot_general | solution.py:162
  248.3 3.8 multiply_reduce_fusion.1
  254.1 9.4 %fusion.70 = f32[3072,768]{1,0:T(8,128)} fusion(bf16[512,3072]{1,0:T(8,128)(2,1)} %get-tuple-element.247, bf16[512,768]{1,0:T(8,128)(2,1)S(1)} %copy-done.28, f32[512,768]{1,0:T(8,128)} %copy-done.8, f32[512]{0:T(512)} %copy-done.53, f32[512]{0:T(512)} %copy-done.54, f32[768]{0:T(1024)} %param.29, f32[512]{0:T(512)} %copy-done.44, ...), kind=kOutput, calls=%fused_computation.113 | convolution fusion | flops 2419458048 | bytes 14953472 | tf_op jit(solution)/shard_map/nf,nd->fd/dot_general | solution.py:168
  264.2 7.1 fusion.81
  271.5 11.3 %all-gather.12.cloned.1.call-done = bf16[2048,768]{1,0:T(8,128)(2,1)} async-done(((bf16[512,768]{1,0:T(8,128)(2,1)}), bf16[2048,768]{1,0:T(8,128)(2,1)}) %all-gather.12.cloned.1.call-update) | async-done | bytes 3145744 | tf_op jit(solution)/shard_map/all_gather | solution.py:178
  282.8 3.1 convolution_convert_fusion
  288.5 149.3 %while.27 = (s32[]{:T(128)}, f32[4,512,3,192]{1,0,3,2:T(4,128)}, bf16[4,512,3,64]{1,3,2,0:T(8,128)(2,1)}, bf16[4,512,3,64]{1,3,2,0:T(8,128)(2,1)}, bf16[4,512,3,...) while((s32[]{:T(128)}, f32[4,512,3,192]{1,0,3,2:T(4,128)}, ...), condition=%wide.region_17.18_spmd, body=%wide.region_15.17_spmd.sunk | while | flops 913897984 | bytes 59351228 | solution.py:215
  289.6 2.4 subtract_exponential_fusion.3
  296.4 2.2 copy.129
  298.6 23.8 %dynamic_update_slice.31 = f32[4,512,3,192]{1,0,3,2:T(4,128)} dynamic-update-slice(f32[4,512,3,192]{1,0,3,2:T(4,128)} %get-tuple-element.405, f32[1,512,3,192]{1,0,3,2:T(1,128)} %copy.129, s32[]{:T(128)} %get-tuple-element.404, s32[]{:T(128)} %constant.75.clone.1..sunk, s32[]{:T(128)} %constant.75.clone.1..sunk, s32[]{:T(128)} %constant.75.clone.1..sunk) | dynamic-update-slice | bytes 2359300 | tf_op jit(solution)/shard_map/while/body/jit(dynamic_update_index_in_dim)/dynamic_update_slice | solution.py:215
  333.7 2.2 copy.129
  335.9 23.6 %dynamic_update_slice.31 = f32[4,512,3,192]{1,0,3,2:T(4,128)} dynamic-update-slice(f32[4,512,3,192]{1,0,3,2:T(4,128)} %get-tuple-element.405, f32[1,512,3,192]{1,0,3,2:T(1,128)} %copy.129, s32[]{:T(128)} %get-tuple-element.404, s32[]{:T(128)} %constant.75.clone.1..sunk, s32[]{:T(128)} %constant.75.clone.1..sunk, s32[]{:T(128)} %constant.75.clone.1..sunk) | dynamic-update-slice | bytes 2359300 | tf_op jit(solution)/shard_map/while/body/jit(dynamic_update_index_in_dim)/dynamic_update_slice | solution.py:215
  370.8 2.2 copy.129
  373.0 23.9 %dynamic_update_slice.31 = f32[4,512,3,192]{1,0,3,2:T(4,128)} dynamic-update-slice(f32[4,512,3,192]{1,0,3,2:T(4,128)} %get-tuple-element.405, f32[1,512,3,192]{1,0,3,2:T(1,128)} %copy.129, s32[]{:T(128)} %get-tuple-element.404, s32[]{:T(128)} %constant.75.clone.1..sunk, s32[]{:T(128)} %constant.75.clone.1..sunk, s32[]{:T(128)} %constant.75.clone.1..sunk) | dynamic-update-slice | bytes 2359300 | tf_op jit(solution)/shard_map/while/body/jit(dynamic_update_index_in_dim)/dynamic_update_slice | solution.py:215
  408.1 2.2 copy.129
  410.4 23.7 %dynamic_update_slice.31 = f32[4,512,3,192]{1,0,3,2:T(4,128)} dynamic-update-slice(f32[4,512,3,192]{1,0,3,2:T(4,128)} %get-tuple-element.405, f32[1,512,3,192]{1,0,3,2:T(1,128)} %copy.129, s32[]{:T(128)} %get-tuple-element.404, s32[]{:T(128)} %constant.75.clone.1..sunk, s32[]{:T(128)} %constant.75.clone.1..sunk, s32[]{:T(128)} %constant.75.clone.1..sunk) | dynamic-update-slice | bytes 2359300 | tf_op jit(solution)/shard_map/while/body/jit(dynamic_update_index_in_dim)/dynamic_update_slice | solution.py:215
  437.9 7.0 reshape.210
  449.1 2.4 subtract_convert_fusion
  455.0 4.6 convolution_bitcast_fusion
  460.8 2.6 fusion.69
  463.4 3.9 fusion.93
  467.3 3.2 fusion.65
  472.5 10.1 %all-reduce = f32[3072]{0:T(1024)S(1)} all-reduce(f32[3072]{0:T(1024)S(1)} %copy-done.39), channel_id=5, replica_groups=mesh['dp'=8,'mp'=4] {'mp'}, use_global_device_ids=true, to_apply=%region_29.30.clone | all-reduce | flops 3072 | bytes 24576
  482.7 40.5 %all-reduce.1 = (f32[768]{0:T(1024)}, f32[768]{0:T(1024)}, f32[768]{0:T(1024)}, f32[768]{0:T(1024)}) all-reduce(f32[768]{0:T(1024)S(1)} %copy-done.49, f32[768]{0:T(1024)S(1)} %copy-done.50, f32[768]{0:T(1024)S(1)} %copy-done.37, f32[768]{0:T(1024)S(1)} %copy-done.38), channel_id=1, replica_groups=mesh['dp'=8,'mp'=4] {'dp','mp'}, use_global_device_ids=true, to_apply=%region_23.24 | all-reduce | flops 3072 | bytes 24576 | tf_op jit(solution)/shard_map/psum | solution.py:248
  523.2 22.2 %psum.76 = f32[768]{0:T(1024)} all-reduce(f32[768]{0:T(1024)S(1)} %dynamic-slice.1), channel_id=1, replica_groups=mesh['dp'=8,'mp'=4] {'dp'}, use_global_device_ids=true, to_apply=%region_30.31 | all-reduce | flops 768 | bytes 6144 | tf_op jit(solution)/shard_map/psum | solution.py:251
  545.4 2.7 add.133
  548.1 216.4 %all-reduce.5.cloned.1.call-done = (f32[768,3,192]{0,2,1:T(8,128)}, f32[128,192]{0,1:T(8,128)}, f32[192,768]{1,0:T(8,128)}, f32[768,768]{1,0:T(8,128)}, f32[768,768]{1,0:T(8,128)}) async-done(((f32[768,3,192]{0,2,1:T(8,128)}, f32[128,192]{0,1:T(8,128)}, f32[192,768]{1,0:T(8,128)}, f32[768,768]{1,0:T(8,128)}, f32[768,768]{1,0:T(8,128)}), (f32[768,3,192]{0,2,1:T(8,128)}, f32[128,192]{0,1:T(8,128)}, ...) | async-done | bytes 7176208 | tf_op jit(solution)/shard_map/psum | solution.py:251
  764.6 2.9 copy.163
  (274 shorter events, 97.7 us)
Async XLA Ops:
  7.2 33.7 %copy-start = (bf16[768,3,192]{0,2,1:T(8,128)(2,1)S(1)}, bf16[768,3,192]{0,2,1:T(8,128)(2,1)}, u32[]{:S(2)}) copy-start(bf16[768,3,192]{0,2,1:T(8,128)(2,1)} %param.21) | copy-start | bytes 2654212
  7.2 11.7 %copy-start.51 = (s32[4,6]{1,0:T(4,128)S(1)}, s32[4,6]{1,0:T(4,128)}, u32[]{:S(2)}) copy-start(s32[4,6]{1,0:T(4,128)} %param.20) | copy-start | bytes 292
  7.2 33.7 %all-gather.6.cloned.1.call-start = ((), (), s32[]{:S(2)}) async-start(), calls=%async_computation.4 | async-start | bytes 3932160 | tf_op jit(solution)/shard_map/all_gather | solution.py:93
  7.9 144.9 %reduce-scatter.5.cloned.1.call-start = ((), (), s32[]{:S(2)}) async-start(), calls=%async_computation.5 | async-start | bytes 7864320 | tf_op jit(solution)/shard_map/reduce_scatter | solution.py:136
  19.9 38.3 %copy-start.12 = (f32[2048,64]{0,1:T(8,128)}, f32[2048,64]{0,1:T(8,128)S(1)}, u32[]{:S(2)}) copy-start(f32[2048,64]{0,1:T(8,128)S(1)} %get-tuple-element.243) | copy-start | bytes 1572868
  19.9 38.3 %copy-start.14 = (f32[2048,64]{0,1:T(8,128)}, f32[2048,64]{0,1:T(8,128)S(1)}, u32[]{:S(2)}) copy-start(f32[2048,64]{0,1:T(8,128)S(1)} %get-tuple-element.244) | copy-start | bytes 1572868
  44.9 12.7 %copy-start.6 = (bf16[2048,1,192]{0,2,1:T(8,128)(2,1)}, bf16[2048,1,192]{0,2,1:T(8,128)(2,1)S(1)}, u32[]{:S(2)}) copy-start(bf16[2048,1,192]{0,2,1:T(8,128)(2,1)S(1)} %slice.70) | copy-start | bytes 2359300
  53.3 4.4 copy-start.33
  87.2 7.1 copy-start.3
  94.3 58.5 %copy-start.16 = (bf16[512,768]{1,0:T(8,128)(2,1)S(1)}, bf16[512,768]{1,0:T(8,128)(2,1)}, u32[]{:S(2)}) copy-start(bf16[512,768]{1,0:T(8,128)(2,1)} %param.18) | copy-start | bytes 2359300
  94.4 97.6 %all-gather.8.cloned.1.call-start = ((), (), s32[]{:S(2)}) async-start(), calls=%async_computation.6 | async-start | bytes 5898240 | tf_op jit(solution)/shard_map/all_gather | solution.py:147
  95.1 135.9 %all-gather.10.cloned.1.call-start = ((), (), s32[]{:S(2)}) async-start(), calls=%async_computation.7 | async-start | bytes 5898240 | tf_op jit(solution)/shard_map/all_gather | solution.py:149
  95.7 187.1 %all-gather.12.cloned.1.call-start = ((), (), s32[]{:S(2)}) async-start(), calls=%async_computation.8 | async-start | bytes 3932160 | tf_op jit(solution)/shard_map/all_gather | solution.py:178
  154.8 76.2 %copy-start.41 = (f32[512]{0:T(512)}, f32[512]{0:T(512)S(1)}, u32[]{:S(2)}) copy-start(f32[512]{0:T(512)S(1)} %add_rsqrt_fusion.1) | copy-start | bytes 6148
  231.0 6.5 copy-start.28
  231.0 6.5 copy-start.45
  231.0 6.6 copy-start.46
  231.0 8.8 %copy-start.60 = (f32[512,3072]{1,0:T(8,128)S(1)}, f32[512,3072]{1,0:T(8,128)}, u32[]{:S(2)}) copy-start(f32[512,3072]{1,0:T(8,128)} %get-tuple-element.248) | copy-start | bytes 18874372
  237.2 11.1 %copy-start.8 = (f32[512,768]{1,0:T(8,128)}, f32[512,768]{1,0:T(8,128)S(1)}, u32[]{:S(2)}) copy-start(f32[512,768]{1,0:T(8,128)S(1)} %get-tuple-element.250) | copy-start | bytes 4718596
  237.5 10.7 %copy-start.44 = (f32[512]{0:T(512)}, f32[512]{0:T(512)S(1)}, u32[]{:S(2)}) copy-start(f32[512]{0:T(512)S(1)} %add_rsqrt_fusion) | copy-start | bytes 6148
  237.6 10.7 %slice-start = ((s8[4718592]{0:T(1024)(128)(4,1)}), s8[4194304]{0:T(1024)(128)(4,1)S(1)}, s32[]{:S(2)}) async-start(s8[4718592]{0:T(1024)(128)(4,1)} %bitcast.211), calls=%async_computation.13 | async-start | bytes 8388608
  239.8 8.5 %copy-start.53 = (f32[512]{0:T(512)}, f32[512]{0:T(512)S(1)}, u32[]{:S(2)}) copy-start(f32[512]{0:T(512)S(1)} %get-tuple-element.254) | copy-start | bytes 6148
  239.8 8.5 %copy-start.54 = (f32[512]{0:T(512)}, f32[512]{0:T(512)S(1)}, u32[]{:S(2)}) copy-start(f32[512]{0:T(512)S(1)} %get-tuple-element.255) | copy-start | bytes 6148
  240.4 7.9 %copy-start.42 = (f32[512]{0:T(512)S(1)}, f32[512]{0:T(512)}, u32[]{:S(2)}) copy-start(f32[512]{0:T(512)} %copy-done.41) | copy-start | bytes 6148
  240.4 7.9 %copy-start.47 = (f32[768]{0:T(1024)S(1)}, f32[768]{0:T(1024)}, u32[]{:S(2)}) copy-start(f32[768]{0:T(1024)} %param.24) | copy-start | bytes 9220
  240.4 7.9 %slice-start.1 = ((s8[4718592]{0:T(1024)(128)(4,1)}), s8[524288]{0:T(1024)(128)(4,1)S(1)}, s32[]{:S(2)}) async-start(s8[4718592]{0:T(1024)(128)(4,1)} %bitcast.211), calls=%async_computation.14 | async-start | bytes 1048576
  248.3 3.9 copy-start.59
  254.1 216.5 %reduce-scatter.11.cloned.1.call-start = ((), (), s32[]{:S(2)}) async-start(), calls=%async_computation.11 | async-start | bytes 11796480 | tf_op jit(solution)/shard_map/reduce_scatter | solution.py:172
  263.5 207.0 %reduce-scatter.9.cloned.1.call-start = ((), (), s32[]{:S(2)}) async-start(), calls=%async_computation.10 | async-start | bytes 11796480 | tf_op jit(solution)/shard_map/reduce_scatter | solution.py:170
  271.4 274.0 %reduce-scatter.7.cloned.1.call-start = ((), (), s32[]{:S(2)}) async-start(), calls=%async_computation.9 | async-start | bytes 7864320 | tf_op jit(solution)/shard_map/reduce_scatter | solution.py:242
  437.9 7.0 copy-start.18
  445.5 3.6 copy-start.13
  445.5 3.5 copy-start.15
  451.4 3.6 copy-start.24
  451.5 3.6 copy-start.26
  459.7 3.7 copy-start.5
  459.7 304.9 %all-reduce.5.cloned.1.call-start = ((), (), s32[]{:S(2)}) async-start(), calls=%async_computation.12 | async-start | bytes 14352384 | tf_op jit(solution)/shard_map/psum | solution.py:251
  460.8 6.5 copy-start.56
  463.4 3.9 copy-start.25
  463.4 3.9 copy-start.27
  463.4 3.9 copy-start.30
  470.6 12.1 %copy-start.37 = (f32[768]{0:T(1024)S(1)}, f32[768]{0:T(1024)}, u32[]{:S(2)}) copy-start(f32[768]{0:T(1024)} %get-tuple-element.179) | copy-start | bytes 9220
  470.6 12.1 %copy-start.38 = (f32[768]{0:T(1024)S(1)}, f32[768]{0:T(1024)}, u32[]{:S(2)}) copy-start(f32[768]{0:T(1024)} %get-tuple-element.184) | copy-start | bytes 9220
  470.6 12.1 %copy-start.49 = (f32[768]{0:T(1024)S(1)}, f32[768]{0:T(1024)}, u32[]{:S(2)}) copy-start(f32[768]{0:T(1024)} %get-tuple-element.177) | copy-start | bytes 9220
  470.6 12.1 %copy-start.50 = (f32[768]{0:T(1024)S(1)}, f32[768]{0:T(1024)}, u32[]{:S(2)}) copy-start(f32[768]{0:T(1024)} %get-tuple-element.182) | copy-start | bytes 9220
  470.6 74.8 %copy-start.9 = (f32[512,768]{1,0:T(8,128)S(1)}, f32[512,768]{1,0:T(8,128)}, u32[]{:S(2)}) copy-start(f32[512,768]{1,0:T(8,128)} %get-tuple-element.229) | copy-start | bytes 4718596
  764.6 3.6 copy-start.31
  764.6 4.4 copy-start.22
  (30 other events, 56.1 us)
Sparse Core Ops, SparseCore 0:
  9.6 31.2 all-gather.5
  94.5 58.3 reduce-scatter.4
  154.5 37.4 all-gather.7
  193.5 37.4 all-gather.9
  254.2 28.5 all-gather.11
  285.4 78.3 reduce-scatter.10
  366.6 78.3 reduce-scatter.8
  459.8 59.1 reduce-scatter.6
  524.6 239.8 all-reduce.4
where the time goes:
time: 793 us; the launch traced here: 780 us
  waiting for transfers between devices  370 us (47%)
  local copies, waits for them, and re-layouts  158 us (20%)
  matrix products  121 us (15%)
  blocking collectives  86.7 us (11%)
  other arithmetic  27.1 us (3%)
  between operations  15.4 us (2%)
    psum x1, waiting for transfers between devices, on_device(): lax.psum((qkv_grad, box_grad, out_grad_weight, up_grad, up_bias_grad, dow...  216 us
    dynamic_update_slice x8, local copies, waits for them, and re-layouts, on_device(): lax.map(attend_back, (query_aug, key_aug, value_slots, page_ids, log_tota...  104 us
    reduce_scatter x1, waiting for transfers between devices, on_device(): lax.psum_scatter(jnp.dot(row_part, out_weight, preferred_element_type=jnp...  51.3 us
    psum x1, blocking collectives, on_device(): lax.psum((gain1_part, bias1_part, gain2_part, bias2_part), ('dp', 'mp'))  40.5 us
    all_gather x1, waiting for transfers between devices, on_device(): lax.all_gather(up_weight, 'mp', axis=1, tiled=True)  37.2 us
    all_gather x1, waiting for transfers between devices, on_device(): lax.all_gather(down_weight, 'mp', axis=0, tiled=True)  30.8 us
    psum x1, blocking collectives, on_device(): lax.psum((qkv_grad, box_grad, out_grad_weight, up_grad, up_bias_grad, dow...  22.2 us
    all_gather x1, waiting for transfers between devices, on_device(): lax.all_gather(hidden_in, 'mp', axis=0, tiled=True)  20.9 us
  transfers between devices with their start and end apart: 9, of which 6 were waited for; matrix products, arithmetic and copies ran while one was open for 28% of the time, Pallas kernels for 0%

commit v1 on v0

v1 whole, which is shorter than its diff:
```python
import functools

import jax
import jax.numpy as jnp
from jax import lax
from jax.experimental import pallas as pl
from jax.experimental.pallas import tpu as pltpu
from jax.sharding import PartitionSpec as P

HEAD_DIM = 64
EPSILON = 1e-05
MASKED = -1000000000.0
ROOT_HALF = 0.7071067811865476
INV_ROOT_TAU = 0.3989422804014327
BF16 = jnp.bfloat16
F32 = jnp.float32


def mm(a, b):
    return jnp.dot(a, b, preferred_element_type=F32)


def mm_t(a, b):
    return lax.dot_general(a, b, (((1,), (1,)), ((), ())), preferred_element_type=F32)


def lanes(n):
    return pl.ds(pl.multiple_of(n, 128), 128)


def half_mask(h, dtype):
    lane = lax.broadcasted_iota(jnp.int32, (1, 128), 1)
    return jnp.where((lane < 64) == (h == 0), 1.0, 0.0).astype(dtype)


MESH = pl.DeviceIdType.MESH


class Wire:
    def __init__(self, send, recv):
        self.send, self.recv, self.count, self.sent = send, recv, 0, []

    def copy(self, src, dst, device):
        i = self.count
        self.count += 1
        made = pltpu.make_async_remote_copy(src_ref=src, dst_ref=dst, send_sem=self.send.at[i], recv_sem=self.recv.at[i],
                                            device_id=device, device_id_type=MESH)
        self.sent.append(made)
        return made

    def settle(self, made):
        made.wait_send()
        self.sent = [other for other in self.sent if other is not made]

    def drain(self):
        for made in self.sent:
            made.wait_send()


class Place:
    def __init__(self):
        dp, mp = lax.axis_index("dp"), lax.axis_index("mp")
        r = lax.rem(dp, 8)
        base = dp - r
        self.y, self.c = lax.div(mp, 2), lax.rem(mp, 2)
        self.z, self.x = lax.div(r, 2), lax.rem(r, 2)
        self.me = mp
        self.part = (dp, self.y * 2 + 1 - self.c)
        self.ynb = (dp, (1 - self.y) * 2 + self.c)
        self.xnb = (base + self.z * 2 + 1 - self.x, mp)
        self.zz = lax.rem(self.z, 2)
        self.znb = (base + (self.z + 1 - 2 * self.zz) * 2 + self.x, mp)
        self.zk = [lax.rem(self.z + k, 4) for k in (1, 2, 3)]
        self.zdev = [(base + k * 2 + self.x, mp) for k in self.zk]
        self.far_part = (1 - self.y) * 2 + 1 - self.c
        self.far_mine = (1 - self.y) * 2 + self.c
        self.near_part = self.y * 2 + 1 - self.c

    def greet(self):
        barrier = pltpu.get_barrier_semaphore()
        for device in [self.part, self.ynb, self.xnb] + self.zdev:
            pl.semaphore_signal(barrier, inc=1, device_id=device, device_id_type=MESH)
        pl.semaphore_wait(barrier, 6)


def rows_of(ref, start, size):
    return ref.at[pl.ds(pl.multiple_of(start, 16), size)]


class Gather:
    def __init__(self, wire, place, own, whole, size):
        self.place = place
        q = size // 4
        at_own = lambda k: own.at[pl.ds(pl.multiple_of(k * q, 16), q)]
        at = lambda j, k: whole(j).at[pl.ds(pl.multiple_of(k * q, 16), q)]

        def half(j, k, h):
            v = at(j, k)
            w = v.shape[-1] // 2
            return v.at[:, pl.ds(h * w, w)]

        x, zz, jy = place.x, place.zz, place.far_mine
        mine, qx, qz, qd = x + 2 * zz, 1 - x + 2 * zz, x + 2 * (1 - zz), 1 - x + 2 * (1 - zz)
        same = lambda v, dev: wire.copy(v, v, dev)
        self.own = wire.copy(own, whole(place.me), place.part)
        self.over = wire.copy(at_own(mine), at(place.me, mine), place.ynb)
        self.fx, self.fz, self.f0 = [same(at(jy, mine), d) for d in (place.xnb, place.znb, place.part)]
        self.dx, self.dz = same(half(jy, qz, 0), place.xnb), same(half(jy, qx, 1), place.znb)
        self.f1, self.f2, self.f3 = [same(at(jy, k), place.part) for k in (qx, qz, qd)]

    def g0(self):
        self.over.start()
        self.own.start()

    def g1(self):
        self.over.wait_recv()
        self.fx.start()
        self.fz.start()
        self.f0.start()

    def g2(self):
        self.fx.wait_recv()
        self.fz.wait_recv()
        self.dx.start()
        self.dz.start()
        self.f1.start()
        self.f2.start()

    def g3(self):
        self.dx.wait_recv()
        self.dz.wait_recv()
        self.f3.start()

    def near(self):
        self.own.wait_recv()

    def far(self):
        for made in (self.f0, self.f1, self.f2, self.f3):
            made.wait_recv()


class SmallGather:
    def __init__(self, wire, place, own, whole):
        self.own = wire.copy(own, whole(place.me), place.part)
        self.over = wire.copy(own, whole(place.me), place.ynb)
        jy = place.far_mine
        self.f0 = wire.copy(whole(jy), whole(jy), place.part)

    def g0(self):
        self.over.start()
        self.own.start()

    def g1(self):
        self.over.wait_recv()
        self.f0.start()

    def near(self):
        self.own.wait_recv()

    def far(self):
        self.f0.wait_recv()


def accumulate(dst, *srcs, out=None):
    rows, cols = dst.shape
    step = next(s for s in (256, 192, 128, 96, 64, 48, 32, 16) if rows % s == 0 and (s * cols <= 24576 or s == 16))

    def one(i, carry):
        rs = pl.ds(pl.multiple_of(i * step, 16), step)
        total = dst[rs, :].astype(F32)
        for s in srcs:
            total = total + s[rs, :].astype(F32)
        (dst if out is None else out)[rs, :] = total.astype(dst.dtype)
        return carry

    lax.fori_loop(0, rows // step, one, 0)


class Reduce:
    def __init__(self, wire, place, grad, rc, ry, rx, rz, split=True):
        self.wire, self.place, self.split = wire, place, split
        mine = grad(place.me)
        rows, cols = mine.shape
        r4, c2 = rows // 4, cols // 2 if split else cols
        cut = (lambda h: pl.ds(pl.multiple_of(h * c2, 128), c2)) if split else (lambda h: slice(None))
        half = lambda v, h: v.at[:, cut(h)]
        piece = lambda v, k: v.at[pl.ds(pl.multiple_of(k * r4, 16), r4), cut(place.x)]
        self.c0 = wire.copy(grad(place.far_part), rc(0), place.part)
        self.c1 = wire.copy(grad(place.near_part), rc(1), place.part)
        self.yc = wire.copy(grad(place.far_mine), ry, place.ynb)
        self.xc = wire.copy(half(mine, 1 - place.x), rx, place.xnb)
        self.zc = [wire.copy(piece(mine, place.zk[k]), rz(k), place.zdev[k]) for k in range(3)]
        own, done = piece(mine, place.z), piece(ry, place.z)
        self.az = [wire.copy(done, done, place.zdev[k]) for k in range(3)]
        mh, dh = half(mine, place.x), half(ry, place.x)
        self.ax = wire.copy(dh, dh, place.xnb) if split else None
        self.done = done
        self.far, self.mine, self.own, self.mh, self.rc, self.ry, self.rx, self.rz = grad(place.far_mine), mine, own, mh, rc, ry, rx, rz

    def s0a(self):
        self.c0.start()

    def s0b(self):
        self.c1.start()

    def s1(self):
        self.c0.wait_recv()
        accumulate(self.far, self.rc(0))
        self.yc.start()

    def s2(self):
        self.c1.wait_recv()
        self.yc.wait_recv()
        accumulate(self.mine, self.rc(1), self.ry)
        self.xc.start()

    def s3(self):
        self.xc.wait_recv()
        if not self.split:
            self.wire.settle(self.xc)
        accumulate(self.mh, self.rx)
        for made in self.zc:
            made.start()

    def s4(self):
        for made in self.zc:
            made.wait_recv()
        accumulate(self.own, *[self.rz(k) for k in range(3)], out=self.done)
        for made in self.az:
            made.start()

    def s5(self):
        for made in self.az:
            made.wait_recv()
        if self.split:
            self.ax.start()

    def s6(self):
        if self.split:
            self.ax.wait_recv()


class SmallReduce:
    def __init__(self, wire, place, grad, rc, ry, rx, rz):
        self.wire, self.place, self.grad, self.rc, self.ry, self.rx, self.rz = wire, place, grad, rc, ry, rx, rz
        self.c0 = wire.copy(grad.at[place.far_part], rc.at[0], place.part)
        self.c1 = wire.copy(grad.at[place.near_part], rc.at[1], place.part)
        self.yc = wire.copy(grad.at[place.far_mine], ry, place.ynb)
        self.xc = wire.copy(grad.at[place.me], rx, place.xnb)
        self.zc = [wire.copy(grad.at[place.me], rz.at[place.z], d) for d in place.zdev]

    def s0a(self):
        self.c0.start()

    def s0b(self):
        self.c1.start()

    def s1(self):
        self.c0.wait_recv()
        j = self.place.far_mine
        self.grad[j] = self.grad[j] + self.rc[0]
        self.yc.start()

    def s2(self):
        self.c1.wait_recv()
        self.yc.wait_recv()
        j = self.place.me
        self.grad[j] = (self.grad[j] + self.rc[1]) + self.ry[...]
        self.xc.start()

    def s3(self):
        self.xc.wait_recv()
        self.wire.settle(self.xc)
        j = self.place.me
        total = self.grad[j] + self.rx[...]
        self.grad[j] = total
        self.rz[self.place.z] = total
        for made in self.zc:
            made.start()

    def s4(self):
        for made in self.zc:
            made.wait_recv()
        for made in self.zc:
            self.wire.settle(made)
        self.grad[self.place.me] = (self.rz[0] + self.rz[1]) + (self.rz[2] + self.rz[3])

    def s5(self):
        pass

    def s6(self):
        pass


def low_half(a, b):
    lane = lax.broadcasted_iota(jnp.int32, a.shape, 1)
    return jnp.where(lane < 64, a, b)


N_COPY = 230


def kernel(x_in, coords, lengths, og_in, q_in, box_in, out_in, up_in, upb_in, dn_in, n1g, n1b, n2g, n2b,
           lo, ig, gq_out, gbox_out, gout_out, gup_out, gdn_out, small_out,
           x, wq, wbox, wout, wup, upb, wdn, gbox, gup, gdn, small,
           feat, sin2, cos2, mask, qp, kp, vp, prob, ctx, hat1, inv1, nl, nlt, actt, slp, br, bg, boxr, do,
           rc_up, rc_dn, ry_up, ry_dn, rx_up, rx_dn, rz_up, rz_dn, rc_q, ry_q, rx_q, rz_q, rc_o, ry_o, rx_o, rz_o,
           rc_b, ry_b, rx_b, rz_b, rc_s, ry_s, rx_s, rz_s, send, recv, local):
    rows, d = x.shape
    n_tile = wup.shape[0]
    loc = q_in.shape[1]
    place = Place()
    me, y = place.me, place.y
    wire = Wire(send, recv)
    near, far = y * 384, (1 - y) * 384

    gq = wup
    gout = wup.at[3]
    dt = actt

    gat_q = [Gather(wire, place, q_in.at[w], lambda j, w=w: wq.at[w, pl.ds(pl.multiple_of(j * loc, 16), loc)], loc) for w in range(3)]
    gat_o = Gather(wire, place, out_in, lambda j: wout.at[pl.ds(pl.multiple_of(j * loc, 16), loc)], loc)
    gat_u = Gather(wire, place, up_in, lambda j: wup.at[j], up_in.shape[0])
    gat_d = Gather(wire, place, dn_in, lambda j: wdn.at[j], dn_in.shape[0])
    gat_b = SmallGather(wire, place, box_in, lambda j: wbox.at[pl.ds(pl.multiple_of(j * loc, 16), loc)])
    gat_s = SmallGather(wire, place, upb_in, lambda j: upb.at[j])
    gathers = gat_q + [gat_b, gat_o, gat_s, gat_u, gat_d]

    ups, dns = [], []
    for s in range(3):
        cs = slice(s * 256, (s + 1) * 256)
        ups.append(Reduce(wire, place, lambda j, cs=cs: gup.at[j, :, cs], lambda i, cs=cs: rc_up.at[i, :, cs], ry_up.at[:, cs],
                          rx_up.at[s], lambda k, s=s: rz_up.at[s, k]))
        dns.append(Reduce(wire, place, lambda j, cs=cs: gdn.at[j, cs], lambda i, cs=cs: rc_dn.at[i, cs], ry_dn.at[cs],
                          rx_dn.at[s], lambda k, s=s: rz_dn.at[s, k]))
    qs = [Reduce(wire, place, lambda j, w=w: gq.at[w, pl.ds(pl.multiple_of(j * loc, 16), loc)], lambda i, w=w: rc_q.at[i, w], ry_q.at[w],
                 rx_q.at[w], lambda k, w=w: rz_q.at[w, k]) for w in range(3)]
    outr = Reduce(wire, place, lambda j: gout.at[pl.ds(pl.multiple_of(j * loc, 16), loc)], lambda i: rc_o.at[i], ry_o, rx_o, lambda k: rz_o.at[k])
    boxs = Reduce(wire, place, lambda j: gbox.at[pl.ds(pl.multiple_of(j * loc, 16), loc)], lambda i: rc_b.at[i], ry_b, rx_b,
                  lambda k: rz_b.at[k], split=False)
    smalls = SmallReduce(wire, place, small, rc_s, ry_s, rx_s, rz_s)
    assert wire.count <= N_COPY
    queue = [[ups[0]], [dns[0]], [ups[1]], [dns[1]], [ups[2]], [dns[2]], [outr, smalls], [qs[0], boxs], [qs[1]], [qs[2]]]

    def step(stage, k):
        if 0 <= k < len(queue):
            for r in queue[k]:
                getattr(r, stage)()

    pairs = [(x_in, x), (og_in, do)]
    pairs += [(q_in.at[w], wq.at[w, pl.ds(pl.multiple_of(me * loc, 16), loc)]) for w in range(3)]
    own_rows = pl.ds(pl.multiple_of(me * loc, 16), loc)
    pairs += [(box_in, wbox.at[own_rows]), (out_in, wout.at[own_rows]), (upb_in, upb.at[me]), (up_in, wup.at[me]), (dn_in, wdn.at[me])]
    loads = [pltpu.make_async_copy(a, b, local.at[i]) for i, (a, b) in enumerate(pairs)]
    for made in loads:
        made.start()

    place.greet()
    for g in gathers:
        g.g0()

    lane = lax.broadcasted_iota(jnp.int32, (rows, 128), 1)
    sub = lax.rem(lane, 64)
    which = lax.div(sub, 16)
    freq = jnp.exp(-jnp.log(10000.0) * lax.rem(sub[:1], 16).astype(F32) / 16)
    c = coords[...].astype(F32)
    angle = jnp.where(which == 0, c[:, 0:1], jnp.where(which == 1, c[:, 1:2], jnp.where(which == 2, c[:, 2:3], c[:, 3:4]))) * freq
    f = jnp.where(lane < 64, jnp.cos(angle), jnp.sin(angle)).astype(BF16)
    feat[...] = f
    f = f.astype(F32)
    rolled = pltpu.roll(f, 64, 1)
    sin2[...] = jnp.where(lane < 64, rolled, f)
    cos2[...] = jnp.where(lane < 64, f, -rolled)
    ends = []
    total = jnp.int32(0)
    for k in range(lengths.shape[1]):
        total = total + lengths[me, k]
        ends.append(total)
    col_pos = lax.broadcasted_iota(jnp.int32, (8, rows), 1)
    col_id = sum([(col_pos >= e).astype(jnp.int32) for e in ends])[:1]
    for r in range(rows // 128):
        row_pos = lax.broadcasted_iota(jnp.int32, (128, rows), 0) + r * 128
        row_id = sum([(row_pos >= e).astype(jnp.int32) for e in ends])
        mask[r * 128:(r + 1) * 128, :] = jnp.where(row_id == col_id, 0.0, MASKED)

    def project(w, dst, first, scale):
        rs = pl.ds(pl.multiple_of(first, 128), 384)
        part = mm_t(x[...], wq[w, rs, :]).astype(BF16)
        if scale != 1.0:
            part = part * jnp.asarray(scale, BF16)
        head = lax.div(first, 128)
        for i in range(3):
            dst[head + i] = part[:, i * 128:(i + 1) * 128]

    def roll_box(first):
        rs = pl.ds(pl.multiple_of(first, 128), 384)
        boxr[rs, :] = pltpu.roll(wbox[rs, :].astype(F32), 64, 1).astype(BF16)

    def attend(pr):
        q = qp[pr]
        keys = jnp.concatenate([kp[pr], feat[...]], axis=1)
        values = vp[pr]
        rs = pl.ds(pl.multiple_of(pr * 128, 128), 128)
        box = jnp.concatenate([wbox[rs, :], boxr[rs, :]], axis=1)
        outs = []
        for h in range(2):
            qm = q * half_mask(h, BF16)
            bt = mm(qm, box)
            rot = (bt[:, :128] * sin2[...] + bt[:, 128:] * cos2[...]).astype(BF16)
            s = mm_t(jnp.concatenate([qm, rot], axis=1), keys) + mask[...]
            e = jnp.exp(s - jnp.max(s, axis=-1, keepdims=True))
            p = (e * (1.0 / jnp.sum(e, axis=-1, keepdims=True))).astype(BF16)
            prob[2 * pr + h] = p
            outs.append(mm(p, values))
        ctx[:, lanes(pr * 128)] = low_half(outs[0], outs[1]).astype(BF16)

    def at(i, steps):
        for k, run in steps.items():
            @pl.when(i == k)
            def _(run=run):
                for s in run:
                    s()

    scale = HEAD_DIM ** -0.5
    loads[0].wait()
    for w, (dst, factor) in enumerate(((qp, scale), (kp, 1.0), (vp, 1.0))):
        loads[2 + w].wait()
        gat_q[w].near()
        project(w, dst, near, factor)
        gat_q[w].g1()
    loads[5].wait()
    gat_b.near()
    gat_b.g1()
    gat_s.g1()
    roll_box(near)

    def attend_near(i, carry):
        attend(lax.div(near, 128) + i)
        at(i, {0: [gat_q[0].g2, gat_o.g1], 1: [gat_q[1].g2, gat_q[2].g2, gat_q[0].g3], 2: [gat_q[1].g3, gat_q[2].g3, gat_u.g1]})
        return carry

    lax.fori_loop(0, 3, attend_near, 0)
    gat_b.far()
    roll_box(far)
    for w, (dst, factor) in enumerate(((qp, scale), (kp, 1.0), (vp, 1.0))):
        gat_q[w].far()
        project(w, dst, far, factor)

    def attend_far(i, carry):
        attend(lax.div(far, 128) + i)
        at(i, {0: [gat_o.g2], 1: [gat_o.g3, gat_d.g1], 2: [gat_u.g2]})
        return carry

    lax.fori_loop(0, 3, attend_far, 0)
    loads[6].wait()
    gat_o.near()
    gat_o.far()

    def norm_one(r, carry):
        rs = pl.ds(pl.multiple_of(r * 256, 256), 256)
        v = mm(ctx[rs, :], wout[...]) + x[rs, :].astype(F32)
        cen = v - jnp.mean(v, axis=-1, keepdims=True)
        inv = lax.rsqrt(jnp.mean(cen * cen, axis=-1, keepdims=True) + EPSILON)
        hat = cen * inv
        hat1[rs, :] = hat
        inv1[rs, :] = jnp.broadcast_to(inv, (256, 128))
        low = (hat * n1g[...] + n1b[...]).astype(BF16)
        nl[rs, :] = low
        return carry

    lax.fori_loop(0, rows // 256, norm_one, 0)
    nlt[...] = nl[...].T

    br[...] = jnp.zeros_like(br)
    for i in (7, 8, 9):
        loads[i].wait()
    gat_s.near()
    gat_u.near()
    gat_d.near()

    def ffn(i, carry):
        at(i, {2: [gat_u.g3, gat_d.g2, gat_s.far, gat_u.far, gat_d.g3, gat_d.far]})
        jy = jnp.where(i < 2, y, 1 - y)
        jc = jnp.where(lax.rem(i, 2) == 0, place.c, 1 - place.c)
        j = jy * 2 + jc
        acts = []
        for s in range(3):
            cs = slice(s * 256, (s + 1) * 256)
            pre = mm(nl[...], wup[j, :, cs]) + upb[j, :1, cs]
            cdf = 0.5 * (1.0 + lax.erf(pre * ROOT_HALF))
            act = (pre * cdf).astype(BF16)
            slp[j, :, cs] = (cdf + pre * jnp.exp(-0.5 * pre * pre) * INV_ROOT_TAU).astype(BF16)
            actt[j, cs, :] = act.T
            acts.append(act)
        br[...] += mm(jnp.concatenate(acts, axis=1), wdn[j])
        return carry

    lax.fori_loop(0, n_tile, ffn, 0)

    small[...] = jnp.zeros_like(small)
    loads[1].wait()

    def norm_two(r, carry):
        rs = pl.ds(pl.multiple_of(r * 128, 128), 128)
        v = hat1[rs, :] * n1g[...] + n1b[...] + br[rs, :]
        cen = v - jnp.mean(v, axis=-1, keepdims=True)
        inv = lax.rsqrt(jnp.mean(cen * cen, axis=-1, keepdims=True) + EPSILON)
        hat = cen * inv
        g = do[rs, :].astype(F32)
        do[rs, :] = (hat * n2g[...] + n2b[...]).astype(BF16)
        w = g * n2g[...]
        back = inv * (w - jnp.mean(w, axis=-1, keepdims=True) - hat * jnp.mean(w * hat, axis=-1, keepdims=True))
        br[rs, :] = back
        bg[rs, :] = back.astype(BF16)
        small[0, 3:4, :] += jnp.sum(g * hat, axis=0, keepdims=True)
        small[0, 4:5, :] += jnp.sum(g, axis=0, keepdims=True)
        return carry

    lax.fori_loop(0, rows // 128, norm_two, 0)
    save_lo = pltpu.make_async_copy(do, lo, local.at[len(loads)])
    save_lo.start()

    def ffn_back(t, carry):
        s = lax.div(t, 4)
        jj = lax.rem(t, 4)
        jy = jnp.where(jj < 2, 1 - y, y)
        jc = jnp.where(lax.rem(jj, 2) == 0, 1 - place.c, place.c)
        j = jy * 2 + jc
        cs = pl.ds(pl.multiple_of(s * 256, 256), 256)
        fg = mm_t(bg[...], wdn[j, cs, :]) * slp[j, :, cs].astype(F32)
        fg = fg.astype(BF16)
        small[j, :1, cs] = jnp.sum(fg.astype(F32), axis=0, keepdims=True)
        slp[j, :, cs] = fg
        gup[j, :, cs] = mm(nlt[...], fg).astype(BF16)
        gdn[j, cs, :] = mm(actt[j, cs, :], bg[...]).astype(BF16)
        steps = {}
        for s in range(3):
            steps[4 * s] = [ups[s].s0a, dns[s].s0a]
            steps[4 * s + 2] = [ups[s].s0b, dns[s].s0b, ups[s].s1, dns[s].s1]
        at(t, steps)
        return carry

    lax.fori_loop(0, 3 * n_tile, ffn_back, 0)

    def ffn_in(j, carry):
        br[...] += mm_t(slp[j], wup[j])
        return carry

    lax.fori_loop(0, n_tile, ffn_in, 0)

    def norm_back(r, carry):
        rs = pl.ds(pl.multiple_of(r * 128, 128), 128)
        up = br[rs, :]
        hat = hat1[rs, :]
        w = up * n1g[...]
        back = inv1[rs, :1] * (w - jnp.mean(w, axis=-1, keepdims=True) - hat * jnp.mean(w * hat, axis=-1, keepdims=True))
        br[rs, :] = back
        bg[rs, :] = back.astype(BF16)
        small[0, 1:2, :] += jnp.sum(up * hat, axis=0, keepdims=True)
        small[0, 2:3, :] += jnp.sum(up, axis=0, keepdims=True)
        return carry

    lax.fori_loop(0, rows // 128, norm_back, 0)
    for j in range(1, n_tile):
        small[j, 1:5, :] = small[0, 1:5, :]
    smalls.s0a()
    smalls.s0b()
    step("s2", 0)

    for made in (gat_u.fx, gat_u.fz, gat_u.f0, gat_u.f1, gat_u.f2, gat_u.dx, gat_u.dz, gat_u.f3):
        wire.settle(made)
    save_lo.wait()
    for t in range(d // 256):
        cs = slice(t * 256, (t + 1) * 256)
        gout[cs, :] = mm(ctx[:, cs].T, bg[...]).astype(BF16)
        do[:, cs] = mm_t(bg[...], wout[cs, :]).astype(BF16)
    outr.s0a()
    outr.s0b()
    smalls.s1()
    step("s3", 0)

    def attend_back(pr):
        q8t = qp[pr].T
        up = do[:, lanes(pr * 128)]
        upt = up.T
        values = vp[pr]
        keys = jnp.concatenate([kp[pr], feat[...]], axis=1)
        rs = pl.ds(pl.multiple_of(pr * 128, 128), 128)
        box = wbox[rs, :]
        dots = up.astype(F32) * ctx[:, lanes(pr * 128)].astype(F32)
        dqs, dks, dvs = [], [], []
        for h in range(2):
            hs = slice(64 * h, 64 * h + 64)
            p = prob[2 * pr + h]
            dot = jnp.sum(dots * half_mask(h, F32), axis=-1, keepdims=True)
            ds = (p.astype(F32) * (mm_t(up * half_mask(h, BF16), values) - dot)).astype(BF16)
            dvs.append(mm(upt[hs], p))
            dks.append(mm(q8t[hs], ds))
            da = mm(ds, keys) * (HEAD_DIM ** -0.5)
            rg = da[:, 128:]
            turn = (rg * sin2[...] - pltpu.roll(rg, 64, 1) * cos2[...]).astype(BF16)
            gbox[pl.ds(pl.multiple_of(pr * 128 + 64 * h, 64), 64), :] = (mm(q8t[hs], turn) * (HEAD_DIM ** 0.5)).astype(BF16)
            dqs.append(da[:, :128] + mm_t(turn, box))
        dq = low_half(dqs[0], dqs[1]).astype(BF16)
        dkt = jnp.concatenate(dks, axis=0).astype(BF16)
        dvt = jnp.concatenate(dvs, axis=0).astype(BF16)
        dt[0, rs, :] = dq.T
        dt[1, rs, :] = dkt
        dt[2, rs, :] = dvt
        qp[pr] = dq
        kp[pr] = dkt.T
        vp[pr] = dvt.T

    def weight_grads(first):
        rs = pl.ds(pl.multiple_of(first, 128), 384)
        for w in range(3):
            gq[w, rs, :] = mm(dt[w, rs, :], x[...]).astype(BF16)

    def attend_back_far(i, carry):
        attend_back(lax.div(far, 128) + i)
        at(i, {0: [outr.s1]})
        return carry

    lax.fori_loop(0, 3, attend_back_far, 0)
    weight_grads(far)
    for r in qs + [boxs]:
        r.s0a()
    step("s2", 1)
    step("s4", 0)

    def attend_back_near(i, carry):
        attend_back(lax.div(near, 128) + i)
        at(i, {0: [qs[0].s1, qs[1].s1, qs[2].s1, boxs.s1], 1: [lambda: step("s3", 1)], 2: [lambda: step("s2", 2), lambda: step("s5", 0)]})
        return carry

    lax.fori_loop(0, 3, attend_back_near, 0)
    weight_grads(near)
    for r in qs + [boxs]:
        r.s0b()
    step("s4", 1)

    for r in range(rows // 256):
        rs = slice(r * 256, (r + 1) * 256)
        acc = br[rs, :]
        for w, src in enumerate((qp, kp, vp)):
            whole = jnp.concatenate([src[i, rs] for i in range(d // 128)], axis=1)
            acc += mm(whole, wq[w])
        br[rs, :] = acc
    save_ig = pltpu.make_async_copy(br, ig, local.at[len(loads) + 1])
    save_ig.start()
    step("s3", 2)
    step("s6", 0)

    for k in range(3, len(queue) + 2):
        step("s2", k)
        step("s5", k - 2)
        step("s4", k - 1)
        step("s3", k)
        step("s6", k - 2)

    ends = [(ry_up, gup_out), (ry_dn, gdn_out), (ry_o, gout_out), (ry_b, gbox_out), (small.at[me], small_out), (ry_q, gq_out)]
    saves = [pltpu.make_async_copy(a, b, local.at[len(loads) + 2 + i]) for i, (a, b) in enumerate(ends)]
    for made in saves:
        made.start()
    wire.drain()
    for made in saves:
        made.wait()
    save_ig.wait()


def on_device(hidden_in, box_coords, page_lengths, qkv_weight, box_weight, out_weight, norm1_gain, norm1_bias,
              up_weight, up_bias, down_weight, norm2_gain, norm2_bias, out_grad):
    rows, d = hidden_in.shape
    n = lax.axis_size("mp")
    loc = qkv_weight.shape[2]
    f = up_weight.shape[1]
    vm = pl.BlockSpec(memory_space=pltpu.VMEM)
    sm = pl.BlockSpec(memory_space=pltpu.SMEM)
    hb = pl.BlockSpec(memory_space=pl.ANY)
    S = jax.ShapeDtypeStruct
    V = pltpu.VMEM
    np_ = d // 128
    D = pltpu.SemaphoreType.DMA
    outs = pl.pallas_call(
        kernel,
        out_shape=[S((rows, d), BF16), S((rows, d), F32), S((3, loc, d), BF16), S((loc, 128), BF16), S((loc, d), BF16),
                   S((d, f), BF16), S((f, d), BF16), S((8, d), F32)],
        in_specs=[hb, vm, sm] + [hb] * 7 + [vm] * 4,
        out_specs=[hb] * 8,
        scratch_shapes=[
            V((rows, d), BF16), V((3, d, d), BF16), V((d, 128), BF16), V((d, d), BF16), V((n, d, f), BF16),
            V((n, 8, d), F32), V((n, f, d), BF16), V((d, 128), BF16), V((n, d, f), BF16), V((n, f, d), BF16), V((n, 8, d), F32),
            V((rows, 128), BF16), V((rows, 128), F32), V((rows, 128), F32), V((rows, rows), F32),
            V((np_, rows, 128), BF16), V((np_, rows, 128), BF16), V((np_, rows, 128), BF16),
            V((d // 64, rows, rows), BF16), V((rows, d), BF16), V((rows, d), F32), V((rows, 128), F32),
            V((rows, d), BF16), V((d, rows), BF16), V((n, f, rows), BF16), V((n, rows, f), BF16),
            V((rows, d), F32), V((rows, d), BF16), V((d, 128), BF16), V((rows, d), BF16),
            V((2, d, f), BF16), V((2, f, d), BF16), V((d, f), BF16), V((f, d), BF16), V((3, d, 128), BF16), V((3, 256, d // 2), BF16),
            V((3, 3, d // 4, 128), BF16), V((3, 3, 64, d // 2), BF16),
            V((2, 3, loc, d), BF16), V((3, loc, d), BF16), V((3, loc, d // 2), BF16), V((3, 3, loc // 4, d // 2), BF16),
            V((2, loc, d), BF16), V((loc, d), BF16), V((loc, d // 2), BF16), V((3, loc // 4, d // 2), BF16),
            V((2, loc, 128), BF16), V((loc, 128), BF16), V((loc, 128), BF16), V((3, loc // 4, 128), BF16),
            V((2, 8, d), F32), V((8, d), F32), V((8, d), F32), V((4, 8, d), F32),
            D((N_COPY,)), D((N_COPY,)), D((24,)),
        ],
        compiler_params=pltpu.CompilerParams(vmem_limit_bytes=67_000_000, collective_id=0, has_side_effects=True),
        name="layer",
    )(hidden_in, box_coords, page_lengths, out_grad, jnp.transpose(qkv_weight, (1, 2, 0)), box_weight.T, out_weight, up_weight,
      jnp.broadcast_to(up_bias.astype(F32)[None], (8, up_bias.shape[0])), down_weight,
      norm1_gain[None], norm1_bias[None], norm2_gain[None], norm2_bias[None])
    lo, ig, gq, gbox, gout, gup, gdn, small = outs
    n_dp = lax.axis_size("dp")
    if n_dp > 8:
        groups = [[g * 8 + i for g in range(n_dp // 8)] for i in range(8)]
        gq, gbox, gout, gup, gdn, small = [
            lax.psum(v.astype(F32), "dp", axis_index_groups=groups) for v in (gq, gbox, gout, gup, gdn, small)]
    up = lambda v: v.astype(F32)
    return (lo, ig, jnp.transpose(up(gq), (2, 0, 1)), up(gbox).T, up(gout), small[1], small[2], up(gup), small[0], up(gdn), small[3], small[4])


def solution(mesh):
    rows = P(("dp", "mp"), None)
    in_specs = (rows, rows, P("dp", None), P(None, None, "mp"), P(None, "mp"), P("mp", None), P(), P(),
                P(None, "mp"), P("mp"), P("mp", None), P(), P(), rows)
    out_specs = (rows, rows, P(None, None, "mp"), P(None, "mp"), P("mp", None), P(), P(),
                 P(None, "mp"), P("mp"), P("mp", None), P(), P())
    return jax.shard_map(on_device, mesh=mesh, in_specs=in_specs, out_specs=out_specs, check_vma=False)
```

time: 793 us -> 209 us (0.26); the launches traced: 780 us -> 208 us
  waiting for transfers between devices: 370 us -> 0 us
  Pallas kernels: 0 us -> 187 us
  local copies, waits for them, and re-layouts: 158 us -> 12.4 us
  matrix products: 121 us -> 0 us
  blocking collectives: 86.7 us -> 0 us
  other arithmetic: 27.1 us -> 7.86 us
  between operations: 15.4 us -> 0.67 us
    psum x1 -> x0, waiting for transfers between devices: 216 us -> none  [on_device(): lax.psum((qkv_grad, box_grad, out_grad_weight, up_grad, up_bias_grad, dow...]
    pallas_call x0 -> x1, Pallas kernels: none -> 187 us  [on_device(): pl.pallas_call(kernel, out_shape=[S((rows, d), BF16), S((rows, d), F32),...]
    dot_general x42 -> x0, matrix products: 117 us -> none  [the longest x8 16.5 us: slot_scores(): jnp.einsum('ihe,jhe->hij', query_block, key_block, preferred_element_type...]
    dynamic_update_slice x8 -> x0, local copies, waits for them, and re-layouts: 104 us -> none  [on_device(): lax.map(attend_back, (query_aug, key_aug, value_slots, page_ids, log_tota...]
    all_gather x4 -> x0, waiting for transfers between devices: 100 us -> none  [the longest x1 37.2 us: on_device(): lax.all_gather(up_weight, 'mp', axis=1, tiled=True)]
    psum x2 -> x0, blocking collectives: 62.7 us -> none  [the longest x1 40.5 us: on_device(): lax.psum((gain1_part, bias1_part, gain2_part, bias2_part), ('dp', 'mp'))]
    reduce_scatter x4 -> x0, waiting for transfers between devices: 51.3 us -> none  [the longest x1 51.3 us: on_device(): lax.psum_scatter(jnp.dot(row_part, out_weight, preferred_element_type=jnp...]
    all_gather x2 -> x0, blocking collectives: 13.8 us -> none  [the longest x1 8.65 us: on_device(): lax.all_gather(features, 'mp', axis=0, tiled=True)]
  transfers between devices with their start and end apart: 9 -> 0, of which waited for: 6 -> 0; matrix products, arithmetic and copies ran while one was open for 28% -> 0% of each run, Pallas kernels for 0% -> 0%
where the time goes in v1:
time: 209 us; the launch traced here: 208 us
  Pallas kernels  187 us (89%)
  local copies, waits for them, and re-layouts  12.4 us (6%)
  other arithmetic  7.86 us (4%)
    pallas_call x1, Pallas kernels, on_device(): pl.pallas_call(kernel, out_shape=[S((rows, d), BF16), S((rows, d), F32),...  187 us
    convert_element_type x3, other arithmetic, on_device(): up = lambda v: v.astype(F32)  5.06 us
    unnamed x13, local copies, waits for them, and re-layouts  4.49 us

profile of v1, /device:TPU:0, one launch (start us, length us, event | category | flops | bytes accessed | tf_op | source)
XLA Modules:
  0.0 208.0 jit_solution(12282747328084409729)
XLA Ops:
  0.6 1.3 broadcast_in_dim.19.n1g
  1.9 1.3 broadcast_in_dim.20.n1b
  3.2 1.3 broadcast_in_dim.21.n2g
  4.4 1.3 broadcast_in_dim.22.n2b
  5.7 1.3 broadcast_in_dim.18.upb_in
  7.0 1.5 copy.26.coords
  8.6 187.1 %layer.1 = (bf16[512,768]{1,0:T(8,128)(2,1)}, f32[512,768]{1,0:T(8,128)}, bf16[3,192,768]{2,1,0:T(8,128)(2,1)}, bf16[192,128]{1,0:T(8,128)(2,1)}, bf16[192,768]{...) custom-call(bf16[512,768]{1,0:T(8,128)(2,1)} %x_in.1, ...), custom_call_target="tpu_custom_call" | custom-call | tf_op jit(solution)/shard_map/layer/pallas_call | solution.py:684
  195.6 0.0 copy-start.3
  195.6 1.6 slice_reduce_fusion
  197.2 1.4 convert_bitcast_fusion.1
  198.7 0.0 copy-start.2
  198.7 1.9 convert_element_type.15
  200.6 0.0 copy-done.3
  200.6 1.4 convert_bitcast_fusion
  201.9 0.0 copy-done.2
  201.9 0.0 copy-start.1
  201.9 1.6 convert_element_type.16
  203.5 0.1 copy-done.1
  203.6 0.0 copy-start.4
  203.6 1.6 convert_element_type.17
  205.2 0.0 copy-done.4
  205.2 0.0 copy-start
  205.2 0.9 copy.29
  206.1 0.8 copy-done
  206.9 1.1 copy.30
Async XLA Ops:
  195.6 5.0 %copy-start.3 = (bf16[3,192,768]{2,1,0:T(8,128)(2,1)S(1)}, bf16[3,192,768]{2,1,0:T(8,128)(2,1)}, u32[]{:S(2)}) copy-start(bf16[3,192,768]{2,1,0:T(8,128)(2,1)} %get-tuple-element.22) | copy-start | bytes 2654212
  198.7 3.3 %copy-start.2 = (bf16[768,768]{1,0:T(8,128)(2,1)S(1)}, bf16[768,768]{1,0:T(8,128)(2,1)}, u32[]{:S(2)}) copy-start(bf16[768,768]{1,0:T(8,128)(2,1)} %get-tuple-element.26) | copy-start | bytes 3538948
  201.9 1.7 copy-start.1
  203.6 1.6 copy-start.4
  205.2 1.7 copy-start
